TPU v7x, 32 devices: a whole 2x2x4 slice. The times are simulated.
32 devices in a mesh: head: 4 (over y, x), blk: 8 (over z, core).
Axes of the slice: x: 2, y: 2, z: 4, core: 2. Of those that a mesh axis runs over, the one named last changes fastest.
Arguments:
- queries: bfloat16 [4096, 2048], P(('blk', 'head')), may hold values from -8 to 8
- keys: bfloat16 [4096, 2048], P(('blk', 'head')), may hold values from -8 to 8
- values: bfloat16 [4096, 2048], P(('blk', 'head')), may hold values from -6 to 6
- grad_out: bfloat16 [4096, 2048], P(('blk', 'head')), may hold values from -6 to 6
- stride_owner: int32 [32, 3], replicated, may hold values from 0 to 7, all different within a row; in each aligned block of 4 rows (0 to 3, 4 to 7, ...) at most 2 rows name the same one
Outputs:
- attended: bfloat16 [4096, 2048], P('blk', 'head')
- grad_queries: bfloat16 [4096, 2048], P('blk', 'head')
- grad_keys: bfloat16 [4096, 2048], P('blk', 'head')
- grad_values: bfloat16 [4096, 2048], P('blk', 'head')
Inputs may be any that keep to these rules, and one draw needn't show every extreme that they name: `stride_owner`: each row names 3 different runs. Within each aligned block of 4 rows no run is named by more than 2 rows, a bound that some block reaches.
All inputs are finite; a program needn't handle non-finite values.
Results may differ from a plain program's by a relative error of at most 0.02.
Values may be sent and summed in bfloat16 or wider, within the bound.
A program may use at most 128 MiB of HBM per device.

v0:
```python
import math
from functools import partial

import jax
import jax.numpy as jnp
from jax import lax
from jax.experimental import pallas as pl
from jax.experimental.pallas import tpu as pltpu
from jax.sharding import PartitionSpec as P

HEAD_DIM = 128
BLOCK = 128
PICKS = 3
MESH = pl.DeviceIdType.MESH


def with_halo(block, sides, width):
    for axis, dim in sides:
        count = lax.axis_size(axis)
        forward = [(i, i + 1) for i in range(count - 1)]
        forward.append((count - 1, 0))
        backward = [(target, source) for source, target in forward]
        low = lax.ppermute(
            lax.slice_in_dim(block, block.shape[dim] - width, None, axis=dim), axis, forward
        )
        high = lax.ppermute(lax.slice_in_dim(block, 0, width, axis=dim), axis, backward)
        block = jnp.concatenate([low, block, high], axis=dim)
    return block


def from_root(block, axis, holder):
    block = jnp.where(lax.axis_index(axis) == holder, block, jnp.zeros_like(block))
    return lax.psum(block, axis)


def slot_tables(stride_owner, n_blk, blocks, capacity, device):
    owner_table = stride_owner.reshape(n_blk, blocks, PICKS)
    owner_ids = jnp.arange(n_blk, dtype=jnp.int32)
    naming = jnp.any(owner_table[:, :, :, None] == owner_ids[None, None, None, :], axis=2)
    counts = naming.astype(jnp.int32)
    ranking = jnp.cumsum(counts, axis=1) - counts
    naming_here = lax.dynamic_index_in_dim(naming, device, 2, keepdims=False)
    ranking_here = lax.dynamic_index_in_dim(ranking, device, 2, keepdims=False)
    slot_ids = jnp.arange(capacity, dtype=jnp.int32)
    matched = naming_here[:, None, :] & (ranking_here[:, None, :] == slot_ids[None, :, None])
    offsets = jnp.sum(
        matched.astype(jnp.int32) * jnp.arange(blocks, dtype=jnp.int32)[None, None, :], axis=2
    )
    own_rows = lax.dynamic_index_in_dim(owner_table, device, 0, keepdims=False)
    own_ranks = lax.dynamic_index_in_dim(ranking, device, 0, keepdims=False)
    picked = jnp.take_along_axis(own_ranks, own_rows, axis=1)
    flat_slot = own_rows * capacity + picked
    return (offsets.reshape(-1), flat_slot, matched.reshape(n_blk * capacity, blocks))


def fetch_keys(stacked, offsets, flat_slot, capacity):
    seq_rows = stacked.shape[1]
    width = stacked.shape[2]
    blocks = seq_rows // BLOCK
    n_blk = lax.axis_size("blk")
    extended = with_halo(stacked, (("blk", 1),), BLOCK)
    extended = extended.reshape(2, blocks + 2, BLOCK, width)
    block_view = stacked.reshape(2, blocks, BLOCK, width)
    leading = from_root(block_view[:, 0:2], "blk", 0)
    outgoing = jnp.take(block_view, offsets, axis=1).reshape(2, n_blk, capacity, BLOCK, width)
    incoming = lax.all_to_all(outgoing, "blk", split_axis=1, concat_axis=1, tiled=True)
    incoming = incoming.reshape(2, n_blk * capacity, BLOCK, width)
    pooled = jnp.concatenate([extended, incoming, leading], axis=1)
    rows_here = jnp.arange(blocks, dtype=jnp.int32)[:, None]
    nearby_index = rows_here + jnp.arange(3, dtype=jnp.int32)[None, :]
    distant_index = blocks + 2 + flat_slot
    leading_index = (
        jnp.zeros((blocks, 2), jnp.int32)
        + (blocks + 2 + n_blk * capacity)
        + jnp.arange(2, dtype=jnp.int32)[None, :]
    )
    table = jnp.concatenate([nearby_index, distant_index, leading_index], axis=1)
    return jnp.take(pooled, table.reshape(-1), axis=1)


def score_block(query_part, key_part, factor):
    return (
        jnp.einsum("gqhd,gjkhd->ghqjk", query_part, key_part, preferred_element_type=jnp.float32)
        * factor
    )


def log_normal(scores):
    row_max = jnp.max(scores, axis=(3, 4), keepdims=True)
    return row_max + jnp.log(jnp.sum(jnp.exp(scores - row_max), axis=(3, 4), keepdims=True))


def output_of(rounded, value_part):
    return jnp.einsum(
        "ghqjk,gjkhd->gqhd", rounded, value_part, preferred_element_type=jnp.float32
    ).astype(jnp.bfloat16)


def split_terms(coeffs, source):
    group_size = source.shape[0]
    near = jnp.einsum(
        "ghqjk,gqhd->gjkhd", coeffs[:, :, :, 0:3], source, preferred_element_type=jnp.float32
    )
    far = jnp.einsum(
        "ghqjk,gqhd->gjkhd", coeffs[:, :, :, 3:6], source, preferred_element_type=jnp.float32
    ).astype(jnp.bfloat16)
    lead = jnp.einsum(
        "ghqjk,gqhd->jkhd", coeffs[:, :, :, 6:8], source, preferred_element_type=jnp.float32
    )
    near = near.reshape(group_size, 3, near.shape[2], near.shape[3] * near.shape[4])
    far = far.reshape(group_size, 3, far.shape[2], far.shape[3] * far.shape[4])
    lead = lead.reshape(2, lead.shape[1], lead.shape[2] * lead.shape[3])
    return (near, far, lead)


def backward_from(
    scores, log_total, rounded, attended, grad_part, query_part, key_part, value_part, factor
):
    grad_weights = jnp.einsum(
        "gqhd,gjkhd->ghqjk", grad_part, value_part, preferred_element_type=jnp.float32
    )
    delta = jnp.sum(grad_part.astype(jnp.float32) * attended.astype(jnp.float32), axis=3)
    delta = jnp.transpose(delta, (0, 2, 1))[:, :, :, None, None]
    grad_scores = (jnp.exp(scores - log_total) * (grad_weights - delta) * factor).astype(
        jnp.bfloat16
    )
    grad_query = jnp.einsum(
        "ghqjk,gjkhd->gqhd", grad_scores, key_part, preferred_element_type=jnp.float32
    ).astype(jnp.bfloat16)
    key_near, key_far, key_lead = split_terms(grad_scores, query_part)
    value_near, value_far, value_lead = split_terms(rounded, grad_part)
    return (grad_query, key_near, key_far, key_lead, value_near, value_far, value_lead)


def spread_near(near_terms, width):
    blank = jnp.zeros((1, BLOCK, width), jnp.float32)
    return (
        jnp.concatenate([near_terms[:, 0], blank, blank], axis=0)
        + jnp.concatenate([blank, near_terms[:, 1], blank], axis=0)
        + jnp.concatenate([blank, blank, near_terms[:, 2]], axis=0)
    )


def by_runs(queries, keys, values, grad_out, stride_owner):
    query_rows, key_rows, value_rows, grad_rows = (
        lax.all_to_all(queries, "head", split_axis=1, concat_axis=0, tiled=True),
        lax.all_to_all(keys, "head", split_axis=1, concat_axis=0, tiled=True),
        lax.all_to_all(values, "head", split_axis=1, concat_axis=0, tiled=True),
        lax.all_to_all(grad_out, "head", split_axis=1, concat_axis=0, tiled=True),
    )
    seq_rows, width = query_rows.shape
    heads_here = width // HEAD_DIM
    blocks = seq_rows // BLOCK
    n_blk = lax.axis_size("blk")
    capacity = max(2, (PICKS * blocks + n_blk - 1) // n_blk)
    device = lax.axis_index("blk")
    offsets, flat_slot, matched = slot_tables(stride_owner, n_blk, blocks, capacity, device)
    group_size = math.gcd(blocks, max(1, 512 // BLOCK))
    group_count = blocks // group_size
    factor = HEAD_DIM ** (-0.5)
    stacked = jnp.stack([key_rows, value_rows])
    query_view = query_rows.reshape(blocks, BLOCK, heads_here, HEAD_DIM)
    grad_view = grad_rows.reshape(blocks, BLOCK, heads_here, HEAD_DIM)
    key_sets = fetch_keys(stacked, offsets, flat_slot, capacity)
    key_sets = key_sets.reshape(2, blocks, 8, BLOCK, heads_here, HEAD_DIM)

    def pieces(group_id):
        start = group_id * group_size
        query_part = lax.dynamic_slice_in_dim(query_view, start, group_size, 0)
        grad_part = lax.dynamic_slice_in_dim(grad_view, start, group_size, 0)
        kv_part = lax.dynamic_slice_in_dim(key_sets, start, group_size, 1)
        return (query_part, grad_part, kv_part[0], kv_part[1])

    def joined_pass(group_id):
        query_part, grad_part, key_part, value_part = pieces(group_id)
        scores = score_block(query_part, key_part, factor)
        log_total = log_normal(scores)
        rounded = jnp.exp(scores - log_total).astype(jnp.bfloat16)
        attended = output_of(rounded, value_part)
        extra = backward_from(
            scores,
            log_total,
            rounded,
            attended,
            grad_part,
            query_part,
            key_part,
            value_part,
            factor,
        )
        return (attended,) + extra

    group_ids = jnp.arange(group_count, dtype=jnp.int32)
    results = lax.map(joined_pass, group_ids)
    attended = results[0]
    grad_query, key_near, key_far, key_lead, value_near, value_far, value_lead = results[1:]
    key_ext = spread_near(key_near.reshape(blocks, 3, BLOCK, width), width)
    value_ext = spread_near(value_near.reshape(blocks, 3, BLOCK, width), width)
    rim_terms = jnp.stack(
        [
            jnp.stack([key_ext[0], value_ext[0]]),
            jnp.stack([key_ext[blocks + 1], value_ext[blocks + 1]]),
        ]
    )
    beside = with_halo(rim_terms.astype(jnp.bfloat16), (("blk", 0),), 1).astype(rim_terms.dtype)
    key_owned = key_ext[1 : blocks + 1].at[0].add(beside[0, 0]).at[blocks - 1].add(beside[3, 0])
    value_owned = value_ext[1 : blocks + 1].at[0].add(beside[0, 1]).at[blocks - 1].add(beside[3, 1])
    slot_flat = flat_slot.reshape(-1)
    key_back = (
        jnp.zeros((n_blk * capacity, BLOCK, width), jnp.bfloat16)
        .at[slot_flat]
        .set(key_far.reshape(blocks * PICKS, BLOCK, width))
    )
    value_back = (
        jnp.zeros((n_blk * capacity, BLOCK, width), jnp.bfloat16)
        .at[slot_flat]
        .set(value_far.reshape(blocks * PICKS, BLOCK, width))
    )
    key_arrived, value_arrived = (
        lax.all_to_all(
            key_back.reshape(n_blk, capacity, BLOCK, width),
            "blk",
            split_axis=0,
            concat_axis=0,
            tiled=True,
        ),
        lax.all_to_all(
            value_back.reshape(n_blk, capacity, BLOCK, width),
            "blk",
            split_axis=0,
            concat_axis=0,
            tiled=True,
        ),
    )
    match_b = matched.astype(jnp.bfloat16)
    key_owned = key_owned + jnp.einsum(
        "sr,sbc->rbc",
        match_b,
        key_arrived.reshape(n_blk * capacity, BLOCK, width),
        preferred_element_type=jnp.float32,
    )
    value_owned = value_owned + jnp.einsum(
        "sr,sbc->rbc",
        match_b,
        value_arrived.reshape(n_blk * capacity, BLOCK, width),
        preferred_element_type=jnp.float32,
    )
    key_total, value_total = (
        lax.psum(jnp.sum(key_lead, axis=0).astype(jnp.bfloat16), "blk").astype(jnp.float32),
        lax.psum(jnp.sum(value_lead, axis=0).astype(jnp.bfloat16), "blk").astype(jnp.float32),
    )
    at_root = device == 0
    key_owned = key_owned.at[0:2].add(jnp.where(at_root, key_total, jnp.zeros_like(key_total)))
    value_owned = value_owned.at[0:2].add(
        jnp.where(at_root, value_total, jnp.zeros_like(value_total))
    )
    grad_keys = key_owned.astype(jnp.bfloat16).reshape(seq_rows, width)
    grad_values = value_owned.astype(jnp.bfloat16).reshape(seq_rows, width)
    return (
        attended.reshape(seq_rows, width),
        grad_query.reshape(seq_rows, width),
        grad_keys,
        grad_values,
    )


def exchange_barrier(peers):
    barrier = pltpu.get_barrier_semaphore()
    for peer in peers:
        pl.semaphore_signal(barrier, inc=1, device_id=peer, device_id_type=MESH)
    pl.semaphore_wait(barrier, len(peers))


def head_kernel(
    n_head,
    n_z,
    owner_in,
    q_in,
    k_in,
    v_in,
    g_in,
    o_out,
    dq_out,
    dk_out,
    dv_out,
    owner_ref,
    q_all,
    k_all,
    v_all,
    g_all,
    k_sum,
    v_sum,
    k_far,
    v_far,
    o_stage,
    dq_stage,
    dk_stage,
    dv_stage,
    k_give,
    v_give,
    k_take,
    v_take,
    in_send,
    in_recv,
    pass_send,
    pass_recv,
    own_sem,
    out_send,
    out_recv,
    out_own,
    pair_send,
    pair_recv,
):
    head = lax.axis_index("head")
    blk = lax.axis_index("blk")
    z = blk // 2
    c = blk % 2
    runs = n_head
    total_blocks = 2 * n_z * runs
    factor = HEAD_DIM ** (-0.5)
    sibling = {"head": head, "blk": 2 * z + 1 - c}
    offsets = [(dz, dh) for dz in range(n_z) for dh in range(n_head)]
    far_first = [dz for dz in (2, 1, 3, 0) if dz < n_z] + list(range(4, n_z))
    near_first = far_first

    def columns(head_id):
        return pl.ds(pl.multiple_of(head_id * HEAD_DIM, HEAD_DIM), HEAD_DIM)

    def to_peer(dz, dh):
        return (z + dz) % n_z, (head + dh) % n_head

    def from_peer(dz, dh):
        return (z + n_z - dz) % n_z, (head + n_head - dh) % n_head

    peers = []
    for dz, dh in offsets:
        if (dz, dh) != (0, 0):
            z2, h2 = to_peer(dz, dh)
            peers.append({"head": h2, "blk": 2 * z2 + c})
    exchange_barrier(peers + [sibling])

    key_pairs = ((0, k_in, k_all), (1, v_in, v_all))
    row_pairs = ((2, q_in, q_all), (3, g_in, g_all))
    mine = blk * runs + head
    my_row = z * runs + head
    my_head = head * n_z + z

    def push(at, source, target, slot, dz, dh):
        z2, h2 = to_peer(dz, dh)
        return pltpu.make_async_remote_copy(
            src_ref=source.at[:, columns(h2 * n_z + z2)],
            dst_ref=target.at[slot],
            send_sem=in_send.at[at, z2 * n_head + h2],
            recv_sem=in_recv.at[at, my_row],
            device_id={"head": h2, "blk": 2 * z2 + c},
            device_id_type=MESH,
        )

    def arrival(at, source, target, slot, dz, dh):
        z1, h1 = from_peer(dz, dh)
        return pltpu.make_async_remote_copy(
            src_ref=source.at[:, columns(my_head)],
            dst_ref=target.at[slot],
            send_sem=in_send.at[at, z1 * n_head + h1],
            recv_sem=in_recv.at[at, z1 * n_head + h1],
            device_id=sibling,
            device_id_type=MESH,
        )

    sends = []
    own_copies = [pltpu.make_async_copy(owner_in, owner_ref, own_sem.at[4])]
    own_copies[0].start()
    for at, source, target in key_pairs:
        own_copies.append(
            pltpu.make_async_copy(
                source.at[:, columns(my_head)], target.at[mine], own_sem.at[at]
            )
        )
        own_copies[-1].start()
    for dz in far_first:
        for dh in range(n_head):
            if (dz, dh) == (0, 0):
                continue
            for at, source, target in key_pairs:
                copy = push(at, source, target, mine, dz, dh)
                copy.start()
                sends.append(copy)
    passes = []
    for at, source, target in key_pairs:
        copy = pltpu.make_async_remote_copy(
            src_ref=source.at[:, columns(my_head)],
            dst_ref=target.at[mine],
            send_sem=pass_send.at[at, my_row],
            recv_sem=pass_recv.at[at, my_row],
            device_id=sibling,
            device_id_type=MESH,
        )
        copy.start()
        passes.append(copy)
    for at, source, target in row_pairs:
        own_copies.append(
            pltpu.make_async_copy(
                source.at[:, columns(my_head)], target.at[my_row], own_sem.at[at]
            )
        )
        own_copies[-1].start()
    for dz in near_first:
        for dh in range(n_head):
            if (dz, dh) == (0, 0):
                continue
            for at, source, target in row_pairs:
                copy = push(at, source, target, my_row, dz, dh)
                copy.start()
                sends.append(copy)

    blank = jnp.zeros((BLOCK, HEAD_DIM), jnp.float32)

    def clear(n, carry):
        k_sum[n] = blank
        v_sum[n] = blank
        return carry

    lax.fori_loop(0, total_blocks, clear, 0)
    none = n_z * runs * PICKS
    k_far[none] = blank.astype(jnp.bfloat16)
    v_far[none] = blank.astype(jnp.bfloat16)

    for dz in [0] + [d for d in far_first if d != 0]:
        for dh in range(n_head):
            if (dz, dh) == (0, 0):
                continue
            z1, h1 = from_peer(dz, dh)
            block = (2 * z1 + c) * runs + h1
            for at, source, target in key_pairs:
                arrival(at, source, target, block, dz, dh).wait_recv()
                copy = pltpu.make_async_remote_copy(
                    src_ref=target.at[block],
                    dst_ref=target.at[block],
                    send_sem=pass_send.at[at, z1 * n_head + h1],
                    recv_sem=pass_recv.at[at, z1 * n_head + h1],
                    device_id=sibling,
                    device_id_type=MESH,
                )
                copy.start()
                passes.append(copy)
    for copy in own_copies:
        copy.wait()
    for row in range(n_z * n_head):
        z1, h1 = row // n_head, row % n_head
        block = (2 * z1 + 1 - c) * runs + h1
        for at, source, target in key_pairs:
            pltpu.make_async_remote_copy(
                src_ref=target.at[block],
                dst_ref=target.at[block],
                send_sem=pass_send.at[at, row],
                recv_sem=pass_recv.at[at, row],
                device_id=sibling,
                device_id_type=MESH,
            ).wait_recv()

    def contract(left, right, dims):
        return lax.dot_general(
            left, right, ((dims[:1], dims[1:]), ((), ())), preferred_element_type=jnp.float32
        )

    def query_step(z1, r):
        row = z1 * runs + r
        block = (2 * z1 + c) * runs + r
        low = (block + total_blocks - 1) % total_blocks
        high = (block + 1) % total_blocks
        picks = [owner_ref[j, block] * runs + r for j in range(PICKS)]
        named = [low, block, high] + picks + [0, 1]
        keys = jnp.concatenate([k_all[n] for n in named], axis=0)
        values = jnp.concatenate([v_all[n] for n in named], axis=0)
        query = q_all[row]
        grad = g_all[row]
        scores = contract(keys, query, (1, 1))
        top = jnp.max(scores, axis=0, keepdims=True)
        weights = jnp.exp((scores - top) * factor)
        weights = weights * (1.0 / jnp.sum(weights, axis=0, keepdims=True))
        rounded = weights.astype(jnp.bfloat16)
        grad_weights = contract(values, grad, (1, 1))
        delta = jnp.sum(weights * grad_weights, axis=0, keepdims=True)
        grad_scores = (weights * (grad_weights - delta) * factor).astype(jnp.bfloat16)
        o_stage[row] = contract(rounded, values, (0, 0)).astype(jnp.bfloat16)
        dq_stage[row] = contract(grad_scores, keys, (0, 0)).astype(jnp.bfloat16)
        key_terms = contract(grad_scores, query, (1, 0))
        value_terms = contract(rounded, grad, (1, 0))
        for j, n in ((0, low), (1, block), (2, high), (6, 0), (7, 1)):
            k_sum[n] += key_terms[j * BLOCK : (j + 1) * BLOCK]
            v_sum[n] += value_terms[j * BLOCK : (j + 1) * BLOCK]
        for j in range(PICKS):
            rows = slice((3 + j) * BLOCK, (4 + j) * BLOCK)
            k_far[row * PICKS + j] = key_terms[rows].astype(jnp.bfloat16)
            v_far[row * PICKS + j] = value_terms[rows].astype(jnp.bfloat16)

    def hand_out(pairs, dz):
        z2 = (z + n_z - dz) % n_z
        for at, stage, out in pairs:
            source = stage.at[pl.ds(z2 * runs, runs)]
            target = out.at[:, :, columns(z)]
            if dz == 0:
                copy = pltpu.make_async_copy(source, target, out_own.at[at])
                copy.start()
                own_outs.append(copy)
            else:
                copy = pltpu.make_async_remote_copy(
                    src_ref=source,
                    dst_ref=target,
                    send_sem=out_send.at[at, z2],
                    recv_sem=out_recv.at[at, z],
                    device_id={"head": head, "blk": 2 * z2 + c},
                    device_id_type=MESH,
                )
                copy.start()
                sends.append(copy)

    own_outs = []
    row_outs = ((0, o_stage, o_out), (1, dq_stage, dq_out))
    key_outs = ((2, dk_stage, dk_out), (3, dv_stage, dv_out))
    for dz in near_first:
        z1 = (z + n_z - dz) % n_z
        for dh in range(n_head):
            if (dz, dh) == (0, 0):
                continue
            h1 = (head + n_head - dh) % n_head
            for at, source, target in row_pairs:
                arrival(at, source, target, z1 * runs + h1, dz, dh).wait_recv()

        def step(r, carry, z1=z1):
            query_step(z1, r)
            return carry

        lax.fori_loop(0, runs, step, 0)
        hand_out(row_outs, dz)

    def total_of(sums, far, run, r):
        total = sums[run * runs + r]
        for z1 in range(n_z):
            block = (2 * z1 + c) * runs + r
            row = z1 * runs + r
            place = none
            for j in range(PICKS):
                place = jnp.where(owner_ref[j, block] == run, row * PICKS + j, place)
            total = total + far[place].astype(jnp.float32)
        return total

    def give_step(row, carry):
        run, r = 2 * (row // runs) + 1 - c, row % runs
        k_give[row] = total_of(k_sum, k_far, run, r).astype(jnp.bfloat16)
        v_give[row] = total_of(v_sum, v_far, run, r).astype(jnp.bfloat16)
        return carry

    lax.fori_loop(0, n_z * runs, give_step, 0)
    pair_copies = []
    for at, give, take in ((0, k_give, k_take), (1, v_give, v_take)):
        copy = pltpu.make_async_remote_copy(
            src_ref=give,
            dst_ref=take,
            send_sem=pair_send.at[at],
            recv_sem=pair_recv.at[at],
            device_id=sibling,
            device_id_type=MESH,
        )
        copy.start()
        pair_copies.append(copy)
    for copy in pair_copies:
        copy.wait_recv()
    for dz in far_first:
        z1 = (z + n_z - dz) % n_z

        def join_step(r, carry, z1=z1):
            row, run = z1 * runs + r, 2 * z1 + c
            for sums, far, take, stage in (
                (k_sum, k_far, k_take, dk_stage),
                (v_sum, v_far, v_take, dv_stage),
            ):
                total = total_of(sums, far, run, r) + take[row].astype(jnp.float32)
                stage[row] = total.astype(jnp.bfloat16)
            return carry

        lax.fori_loop(0, runs, join_step, 0)
        hand_out(key_outs, dz)

    for dz in range(1, n_z):
        z1 = (z + n_z - dz) % n_z
        for at, stage, out in row_outs + key_outs:
            pltpu.make_async_remote_copy(
                src_ref=stage.at[pl.ds(z1 * runs, runs)],
                dst_ref=out.at[:, :, columns(z1)],
                send_sem=out_send.at[at, z1],
                recv_sem=out_recv.at[at, z1],
                device_id=sibling,
                device_id_type=MESH,
            ).wait_recv()
    for copy in own_outs:
        copy.wait()
    for copy in sends + passes + pair_copies:
        copy.wait_send()


def settle_kernel(count, pieces, *refs):
    sources, targets = refs[:count], refs[count : 2 * count]
    held, in_sem, out_sem = refs[2 * count :]
    loads, stores = [], []
    for at in range(count):
        for piece in range(pieces):
            loads.append(
                pltpu.make_async_copy(
                    sources[at].at[piece], held.at[at, piece], in_sem.at[at, piece]
                )
            )
            stores.append(
                pltpu.make_async_copy(
                    held.at[at, piece], targets[at].at[piece], out_sem.at[at, piece]
                )
            )
    for load in loads:
        load.start()
    for load, store in zip(loads, stores):
        load.wait()
        store.start(priority=1)
    for store in stores:
        store.wait()


def by_heads(queries, keys, values, grad_out, stride_owner):
    n_head, n_blk = lax.axis_size("head"), lax.axis_size("blk")
    n_z = n_blk // 2
    rows = n_z * n_head
    seq_rows, width = BLOCK * n_head, n_z * HEAD_DIM
    tile = (BLOCK, HEAD_DIM)
    low, wide = jnp.bfloat16, jnp.float32
    dma = pltpu.SemaphoreType.DMA
    out = jax.ShapeDtypeStruct((n_head, BLOCK, width), low)
    anywhere = pl.BlockSpec(memory_space=pl.ANY)
    arrived = pl.pallas_call(
        partial(head_kernel, n_head, n_z),
        out_shape=(out,) * 4,
        in_specs=[pl.BlockSpec(memory_space=pltpu.HBM)] * 5,
        out_specs=(anywhere,) * 4,
        scratch_shapes=[
            pltpu.SMEM(stride_owner.shape[::-1], jnp.int32),
            pltpu.VMEM((rows,) + tile, low),
            pltpu.VMEM((2 * rows,) + tile, low),
            pltpu.VMEM((2 * rows,) + tile, low),
            pltpu.VMEM((rows,) + tile, low),
            pltpu.VMEM((2 * rows,) + tile, wide),
            pltpu.VMEM((2 * rows,) + tile, wide),
            pltpu.VMEM((rows * PICKS + 1,) + tile, low),
            pltpu.VMEM((rows * PICKS + 1,) + tile, low),
        ]
        + [pltpu.VMEM((rows,) + tile, low)] * 8
        + [
            dma((4, rows)),
            dma((4, rows)),
            dma((2, rows)),
            dma((2, rows)),
            dma((5,)),
            dma((4, n_z)),
            dma((4, n_z)),
            dma((4,)),
            dma((2,)),
            dma((2,)),
        ],
        compiler_params=pltpu.CompilerParams(
            collective_id=0, has_side_effects=True, vmem_limit_bytes=67043328
        ),
    )(stride_owner.T, queries, keys, values, grad_out)
    settled = pl.pallas_call(
        partial(settle_kernel, 4, n_head),
        out_shape=(out,) * 4,
        in_specs=[pl.BlockSpec(memory_space=pl.ANY)] * 4,
        out_specs=(pl.BlockSpec(memory_space=pl.ANY),) * 4,
        scratch_shapes=[
            pltpu.VMEM((4, n_head, BLOCK, width), low),
            dma((4, n_head)),
            dma((4, n_head)),
        ],
        compiler_params=pltpu.CompilerParams(vmem_limit_bytes=67043328),
    )(*arrived)
    return tuple(part.reshape(seq_rows, width) for part in settled)


def on_device(queries, keys, values, grad_out, stride_owner):
    n_head, n_blk = lax.axis_size("head"), lax.axis_size("blk")
    rows, width = queries.shape
    if rows == BLOCK and n_blk % 2 == 0 and width == n_head * (n_blk // 2) * HEAD_DIM:
        return by_heads(queries, keys, values, grad_out, stride_owner)
    return by_runs(queries, keys, values, grad_out, stride_owner)


def solution(mesh):
    return jax.shard_map(
        on_device,
        mesh=mesh,
        in_specs=(
            P(("blk", "head"), None),
            P(("blk", "head"), None),
            P(("blk", "head"), None),
            P(("blk", "head"), None),
            P(),
        ),
        out_specs=(P("blk", "head"), P("blk", "head"), P("blk", "head"), P("blk", "head")),
        check_vma=False,
    )
```

profile of v0, /device:TPU:9, one launch (start us, length us, event | category | flops | bytes accessed | tf_op | source)
XLA Modules:
  0.0 101.7 jit_solution(18050954632401376619)
XLA Ops:
  0.6 98.5 %shard_map.84 = (bf16[4,128,512]{2,1,0:T(8,128)(2,1)}, bf16[4,128,512]{2,1,0:T(8,128)(2,1)}, bf16[4,128,512]{2,1,0:T(8,128)(2,1)}, bf16[4,128,512]{2,1,0:T(8,128)(2,1)}) custom-call(s32[3,32]{1,0:T(4,128)} %bitcast.5, bf16[128,2048]{1,0:T(8,128)(2,1)} %q_in.1, bf16[128,2048]{1,0:T(8,128)(2,1)} %k_in.1, bf16[128,2048]{1,0:T(8,128)(2,1)} %v_in.1, ...), custom_call_target="tpu_custom_call" | custom-call | tf_op jit(solution)/shard_map/pallas_call | solution.py:637
  99.1 2.6 %shard_map.85 = (bf16[4,128,512]{2,1,0:T(8,128)(2,1)}, bf16[4,128,512]{2,1,0:T(8,128)(2,1)}, bf16[4,128,512]{2,1,0:T(8,128)(2,1)}, bf16[4,128,512]{2,1,0:T(8,128)(2,1)}) custom-call(bf16[4,128,512]{2,1,0:T(8,128)(2,1)} %get-tuple-element.12.refs_0_, bf16[4,128,512]{2,1,0:T(8,128)(2,1)} %get-tuple-element.13.refs_1_, ...), custom_call_target="tpu_custom_call" | custom-call | tf_op jit(solution)/shard_map/pallas_call | solution.py:670
where the time goes:
time: 102 us
  Pallas kernels  101 us (99%)
    pallas_call x1, Pallas kernels, by_heads(): pl.pallas_call(partial(head_kernel, n_head, n_z), out_shape=(out,) * 4, i...  98.5 us
    pallas_call x1, Pallas kernels, by_heads(): pl.pallas_call(partial(settle_kernel, 4, n_head), out_shape=(out,) * 4, i...  2.57 us

commit v1 on v0

--- a/solution.py
+++ b/solution.py
@@ -264,13 +264,6 @@
     )
 
 
-def exchange_barrier(peers):
-    barrier = pltpu.get_barrier_semaphore()
-    for peer in peers:
-        pl.semaphore_signal(barrier, inc=1, device_id=peer, device_id_type=MESH)
-    pl.semaphore_wait(barrier, len(peers))
-
-
 def head_kernel(
     n_head,
     n_z,
@@ -279,37 +272,30 @@
     k_in,
     v_in,
     g_in,
-    o_out,
-    dq_out,
-    dk_out,
-    dv_out,
+    out,
     owner_ref,
-    q_all,
-    k_all,
-    v_all,
-    g_all,
+    kv_all,
+    qg_all,
     k_sum,
     v_sum,
     k_far,
     v_far,
-    o_stage,
-    dq_stage,
-    dk_stage,
-    dv_stage,
-    k_give,
-    v_give,
-    k_take,
-    v_take,
-    in_send,
-    in_recv,
+    stage,
+    give,
+    take,
+    owner_sem,
+    kv_send,
+    kv_recv,
+    qg_send,
+    qg_recv,
     pass_send,
     pass_recv,
-    own_sem,
-    out_send,
-    out_recv,
-    out_own,
     pair_send,
     pair_recv,
+    row_send,
+    key_send,
+    out_recv,
+    near_sem,
 ):
     head = lax.axis_index("head")
     blk = lax.axis_index("blk")
@@ -318,145 +304,157 @@
     runs = n_head
     total_blocks = 2 * n_z * runs
     factor = HEAD_DIM ** (-0.5)
+    my_head = head * n_z + z
+    mine = blk * runs + head
+    my_row = z * runs + head
     sibling = {"head": head, "blk": 2 * z + 1 - c}
-    offsets = [(dz, dh) for dz in range(n_z) for dh in range(n_head)]
-    far_first = [dz for dz in (2, 1, 3, 0) if dz < n_z] + list(range(4, n_z))
-    near_first = far_first
 
     def columns(head_id):
         return pl.ds(pl.multiple_of(head_id * HEAD_DIM, HEAD_DIM), HEAD_DIM)
 
-    def to_peer(dz, dh):
-        return (z + dz) % n_z, (head + dh) % n_head
-
-    def from_peer(dz, dh):
-        return (z + n_z - dz) % n_z, (head + n_head - dh) % n_head
-
-    peers = []
-    for dz, dh in offsets:
-        if (dz, dh) != (0, 0):
-            z2, h2 = to_peer(dz, dh)
-            peers.append({"head": h2, "blk": 2 * z2 + c})
-    exchange_barrier(peers + [sibling])
-
-    key_pairs = ((0, k_in, k_all), (1, v_in, v_all))
-    row_pairs = ((2, q_in, q_all), (3, g_in, g_all))
-    mine = blk * runs + head
-    my_row = z * runs + head
-    my_head = head * n_z + z
-
-    def push(at, source, target, slot, dz, dh):
-        z2, h2 = to_peer(dz, dh)
-        return pltpu.make_async_remote_copy(
+    bits = [1 << b for b in range(n_head.bit_length() - 1)]
+
+    def greet(sem):
+        for flip in bits:
+            pl.semaphore_signal(
+                sem,
+                inc=1,
+                device_id={"head": flipped(head, flip), "blk": blk},
+                device_id_type=MESH,
+            )
+        pl.semaphore_signal(sem, inc=1, device_id=sibling, device_id_type=MESH)
+
+        @pl.when(z > 0)
+        def _():
+            pl.semaphore_signal(
+                sem, inc=1, device_id={"head": head, "blk": blk - 2}, device_id_type=MESH
+            )
+
+        @pl.when(z < n_z - 1)
+        def _():
+            pl.semaphore_signal(
+                sem, inc=1, device_id={"head": head, "blk": blk + 2}, device_id_type=MESH
+            )
+
+    def flipped(head_id, flips):
+        moved = head_id
+        for flip in bits:
+            if flips & flip:
+                moved = moved + flip - 2 * flip * ((head_id // flip) % 2)
+        return moved
+
+    def hear(sem):
+        ends = len(bits) + 1 + (z > 0).astype(jnp.int32) + (z < n_z - 1).astype(jnp.int32)
+        pl.semaphore_wait(sem, ends)
+
+    barrier = pltpu.get_barrier_semaphore()
+    greet(barrier)
+
+    local = [pltpu.make_async_copy(owner_in, owner_ref, owner_sem.at[0])]
+    for at, source in enumerate((k_in, v_in)):
+        local.append(
+            pltpu.make_async_copy(
+                source.at[:, columns(my_head)], kv_all.at[at, mine], kv_recv.at[0]
+            )
+        )
+    for at, source in enumerate((q_in, g_in)):
+        local.append(
+            pltpu.make_async_copy(
+                source.at[:, columns(my_head)], qg_all.at[at, my_row], qg_recv.at[0]
+            )
+        )
+    for copy in local:
+        copy.start()
+
+    def push(at, source, target, slot, send_sem, recv_sem, z2, flips):
+        h2 = flipped(head, flips)
+        pltpu.make_async_remote_copy(
             src_ref=source.at[:, columns(h2 * n_z + z2)],
-            dst_ref=target.at[slot],
-            send_sem=in_send.at[at, z2 * n_head + h2],
-            recv_sem=in_recv.at[at, my_row],
+            dst_ref=target.at[at, slot],
+            send_sem=send_sem.at[0],
+            recv_sem=recv_sem,
             device_id={"head": h2, "blk": 2 * z2 + c},
             device_id_type=MESH,
-        )
-
-    def arrival(at, source, target, slot, dz, dh):
-        z1, h1 = from_peer(dz, dh)
-        return pltpu.make_async_remote_copy(
-            src_ref=source.at[:, columns(my_head)],
-            dst_ref=target.at[slot],
-            send_sem=in_send.at[at, z1 * n_head + h1],
-            recv_sem=in_recv.at[at, z1 * n_head + h1],
+        ).start()
+
+    def push_pair(sources, target, slot, send_sem, recv_sem, dz, flips):
+        for sign in (1, -1) if dz else (1,):
+            z2 = z + sign * dz
+
+            @pl.when((z2 >= 0) & (z2 < n_z))
+            def _(z2=z2):
+                arrive = recv_sem.at[(z2 + n_z - z) % n_z]
+                for at, source in enumerate(sources):
+                    push(at, source, target, slot, send_sem, arrive, z2, flips)
+
+    def hops(flips):
+        return sum(1 for flip in bits if flips & flip)
+
+    everyone = sorted(
+        (dz + hops(flips), -dz, flips)
+        for dz in range(n_z)
+        for flips in range(n_head)
+        if dz + hops(flips) > 0
+    )
+    rounds = n_z - 1 + len(bits)
+    for distance in range(1, rounds + 1):
+        if distance == 1:
+            hear(barrier)
+        else:
+            hear(near_sem.at[distance - 2])
+        if distance < rounds:
+            greet(near_sem.at[distance - 1])
+        for hop, minus, flips in everyone:
+            if hop == distance:
+                push_pair((k_in, v_in), kv_all, mine, kv_send, kv_recv, -minus, flips)
+    for dz in [n_z // 2] + [d for d in range(n_z - 1, -1, -1) if d != n_z // 2]:
+        for flips in range(n_head):
+            if dz + hops(flips) > 0:
+                push_pair((q_in, g_in), qg_all, my_row, qg_send, qg_recv, dz, flips)
+
+    blank = jnp.zeros((BLOCK, HEAD_DIM), jnp.float32)
+
+    def clear(n, carry):
+        k_sum[n] = blank
+        v_sum[n] = blank
+        return carry
+
+    lax.fori_loop(0, total_blocks, clear, 0)
+    none = n_z * runs * PICKS
+    k_far[none] = blank.astype(jnp.bfloat16)
+    v_far[none] = blank.astype(jnp.bfloat16)
+
+    def await_bytes(ref, sem):
+        pltpu.make_async_remote_copy(
+            src_ref=ref,
+            dst_ref=ref,
+            send_sem=sem,
+            recv_sem=sem,
             device_id=sibling,
             device_id_type=MESH,
-        )
-
-    sends = []
-    own_copies = [pltpu.make_async_copy(owner_in, owner_ref, own_sem.at[4])]
-    own_copies[0].start()
-    for at, source, target in key_pairs:
-        own_copies.append(
-            pltpu.make_async_copy(
-                source.at[:, columns(my_head)], target.at[mine], own_sem.at[at]
-            )
-        )
-        own_copies[-1].start()
-    for dz in far_first:
-        for dh in range(n_head):
-            if (dz, dh) == (0, 0):
-                continue
-            for at, source, target in key_pairs:
-                copy = push(at, source, target, mine, dz, dh)
-                copy.start()
-                sends.append(copy)
+        ).wait_recv()
+
+    def run_of(dz, core):
+        return 2 * ((z + n_z - dz) % n_z) + core
+
     passes = []
-    for at, source, target in key_pairs:
+    order = [0, 1, n_z - 1] + list(range(2, n_z - 1))
+    for dz in order[:n_z]:
+        group = kv_all.at[:, pl.ds(run_of(dz, c) * runs, runs)]
+        await_bytes(group, kv_recv.at[dz])
         copy = pltpu.make_async_remote_copy(
-            src_ref=source.at[:, columns(my_head)],
-            dst_ref=target.at[mine],
-            send_sem=pass_send.at[at, my_row],
-            recv_sem=pass_recv.at[at, my_row],
+            src_ref=group,
+            dst_ref=group,
+            send_sem=pass_send.at[dz],
+            recv_sem=pass_recv.at[dz],
             device_id=sibling,
             device_id_type=MESH,
         )
         copy.start()
         passes.append(copy)
-    for at, source, target in row_pairs:
-        own_copies.append(
-            pltpu.make_async_copy(
-                source.at[:, columns(my_head)], target.at[my_row], own_sem.at[at]
-            )
-        )
-        own_copies[-1].start()
-    for dz in near_first:
-        for dh in range(n_head):
-            if (dz, dh) == (0, 0):
-                continue
-            for at, source, target in row_pairs:
-                copy = push(at, source, target, my_row, dz, dh)
-                copy.start()
-                sends.append(copy)
-
-    blank = jnp.zeros((BLOCK, HEAD_DIM), jnp.float32)
-
-    def clear(n, carry):
-        k_sum[n] = blank
-        v_sum[n] = blank
-        return carry
-
-    lax.fori_loop(0, total_blocks, clear, 0)
-    none = n_z * runs * PICKS
-    k_far[none] = blank.astype(jnp.bfloat16)
-    v_far[none] = blank.astype(jnp.bfloat16)
-
-    for dz in [0] + [d for d in far_first if d != 0]:
-        for dh in range(n_head):
-            if (dz, dh) == (0, 0):
-                continue
-            z1, h1 = from_peer(dz, dh)
-            block = (2 * z1 + c) * runs + h1
-            for at, source, target in key_pairs:
-                arrival(at, source, target, block, dz, dh).wait_recv()
-                copy = pltpu.make_async_remote_copy(
-                    src_ref=target.at[block],
-                    dst_ref=target.at[block],
-                    send_sem=pass_send.at[at, z1 * n_head + h1],
-                    recv_sem=pass_recv.at[at, z1 * n_head + h1],
-                    device_id=sibling,
-                    device_id_type=MESH,
-                )
-                copy.start()
-                passes.append(copy)
-    for copy in own_copies:
-        copy.wait()
-    for row in range(n_z * n_head):
-        z1, h1 = row // n_head, row % n_head
-        block = (2 * z1 + 1 - c) * runs + h1
-        for at, source, target in key_pairs:
-            pltpu.make_async_remote_copy(
-                src_ref=target.at[block],
-                dst_ref=target.at[block],
-                send_sem=pass_send.at[at, row],
-                recv_sem=pass_recv.at[at, row],
-                device_id=sibling,
-                device_id_type=MESH,
-            ).wait_recv()
+    local[0].wait()
+    for dz in range(n_z):
+        await_bytes(kv_all.at[:, pl.ds(run_of(dz, 1 - c) * runs, runs)], pass_recv.at[dz])
 
     def contract(left, right, dims):
         return lax.dot_general(
@@ -470,10 +468,10 @@
         high = (block + 1) % total_blocks
         picks = [owner_ref[j, block] * runs + r for j in range(PICKS)]
         named = [low, block, high] + picks + [0, 1]
-        keys = jnp.concatenate([k_all[n] for n in named], axis=0)
-        values = jnp.concatenate([v_all[n] for n in named], axis=0)
-        query = q_all[row]
-        grad = g_all[row]
+        keys = jnp.concatenate([kv_all[0, n] for n in named], axis=0)
+        values = jnp.concatenate([kv_all[1, n] for n in named], axis=0)
+        query = qg_all[0, row]
+        grad = qg_all[1, row]
         scores = contract(keys, query, (1, 1))
         top = jnp.max(scores, axis=0, keepdims=True)
         weights = jnp.exp((scores - top) * factor)
@@ -482,8 +480,8 @@
         grad_weights = contract(values, grad, (1, 1))
         delta = jnp.sum(weights * grad_weights, axis=0, keepdims=True)
         grad_scores = (weights * (grad_weights - delta) * factor).astype(jnp.bfloat16)
-        o_stage[row] = contract(rounded, values, (0, 0)).astype(jnp.bfloat16)
-        dq_stage[row] = contract(grad_scores, keys, (0, 0)).astype(jnp.bfloat16)
+        stage[0, row] = contract(rounded, values, (0, 0)).astype(jnp.bfloat16)
+        stage[1, row] = contract(grad_scores, keys, (0, 0)).astype(jnp.bfloat16)
         key_terms = contract(grad_scores, query, (1, 0))
         value_terms = contract(rounded, grad, (1, 0))
         for j, n in ((0, low), (1, block), (2, high), (6, 0), (7, 1)):
@@ -494,45 +492,33 @@
             k_far[row * PICKS + j] = key_terms[rows].astype(jnp.bfloat16)
             v_far[row * PICKS + j] = value_terms[rows].astype(jnp.bfloat16)
 
-    def hand_out(pairs, dz):
+    def hand_out(first, send_sem, dz):
         z2 = (z + n_z - dz) % n_z
-        for at, stage, out in pairs:
-            source = stage.at[pl.ds(z2 * runs, runs)]
-            target = out.at[:, :, columns(z)]
-            if dz == 0:
-                copy = pltpu.make_async_copy(source, target, out_own.at[at])
-                copy.start()
-                own_outs.append(copy)
-            else:
-                copy = pltpu.make_async_remote_copy(
-                    src_ref=source,
-                    dst_ref=target,
-                    send_sem=out_send.at[at, z2],
-                    recv_sem=out_recv.at[at, z],
-                    device_id={"head": head, "blk": 2 * z2 + c},
-                    device_id_type=MESH,
-                )
-                copy.start()
-                sends.append(copy)
-
-    own_outs = []
-    row_outs = ((0, o_stage, o_out), (1, dq_stage, dq_out))
-    key_outs = ((2, dk_stage, dk_out), (3, dv_stage, dv_out))
-    for dz in near_first:
+        source = stage.at[pl.ds(first, 2), pl.ds(z2 * runs, runs)]
+        target = out.at[pl.ds(first, 2), :, :, columns(z)]
+        if dz == 0:
+            pltpu.make_async_copy(source, target, out_recv.at[0]).start()
+        else:
+            pltpu.make_async_remote_copy(
+                src_ref=source,
+                dst_ref=target,
+                send_sem=send_sem.at[0],
+                recv_sem=out_recv.at[0],
+                device_id={"head": head, "blk": 2 * z2 + c},
+                device_id_type=MESH,
+            ).start()
+
+    far_first = [dz for dz in (2, 1, 3, 0) if dz < n_z] + list(range(4, n_z))
+    for dz in far_first:
         z1 = (z + n_z - dz) % n_z
-        for dh in range(n_head):
-            if (dz, dh) == (0, 0):
-                continue
-            h1 = (head + n_head - dh) % n_head
-            for at, source, target in row_pairs:
-                arrival(at, source, target, z1 * runs + h1, dz, dh).wait_recv()
+        await_bytes(qg_all.at[:, pl.ds(z1 * runs, runs)], qg_recv.at[dz])
 
         def step(r, carry, z1=z1):
             query_step(z1, r)
             return carry
 
         lax.fori_loop(0, runs, step, 0)
-        hand_out(row_outs, dz)
+        hand_out(0, row_send, dz)
 
     def total_of(sums, far, run, r):
         total = sums[run * runs + r]
@@ -547,145 +533,131 @@
 
     def give_step(row, carry):
         run, r = 2 * (row // runs) + 1 - c, row % runs
-        k_give[row] = total_of(k_sum, k_far, run, r).astype(jnp.bfloat16)
-        v_give[row] = total_of(v_sum, v_far, run, r).astype(jnp.bfloat16)
+        give[0, row] = total_of(k_sum, k_far, run, r).astype(jnp.bfloat16)
+        give[1, row] = total_of(v_sum, v_far, run, r).astype(jnp.bfloat16)
         return carry
 
     lax.fori_loop(0, n_z * runs, give_step, 0)
-    pair_copies = []
-    for at, give, take in ((0, k_give, k_take), (1, v_give, v_take)):
-        copy = pltpu.make_async_remote_copy(
-            src_ref=give,
-            dst_ref=take,
-            send_sem=pair_send.at[at],
-            recv_sem=pair_recv.at[at],
+    pair = pltpu.make_async_remote_copy(
+        src_ref=give,
+        dst_ref=take,
+        send_sem=pair_send.at[0],
+        recv_sem=pair_recv.at[0],
+        device_id=sibling,
+        device_id_type=MESH,
+    )
+    pair.start()
+    pair.wait_recv()
+    for dz in far_first:
+        z1 = (z + n_z - dz) % n_z
+
+        def join_step(r, carry, z1=z1):
+            row, run = z1 * runs + r, 2 * z1 + c
+            for at, sums, far in ((0, k_sum, k_far), (1, v_sum, v_far)):
+                total = total_of(sums, far, run, r) + take[at, row].astype(jnp.float32)
+                stage[2 + at, row] = total.astype(jnp.bfloat16)
+            return carry
+
+        lax.fori_loop(0, runs, join_step, 0)
+        hand_out(2, key_send, dz)
+
+    def await_sent(ref, sem):
+        pltpu.make_async_remote_copy(
+            src_ref=ref,
+            dst_ref=ref,
+            send_sem=sem,
+            recv_sem=sem,
             device_id=sibling,
             device_id_type=MESH,
+        ).wait_send()
+
+    rows = n_z * runs
+    for copy in passes + [pair]:
+        copy.wait_send()
+    await_sent(kv_all.at[:, pl.ds(0, rows - 1)], kv_send.at[0])
+    await_sent(qg_all.at[:, pl.ds(0, rows - 1)], qg_send.at[0])
+    if n_z > 1:
+        for send_sem in (row_send, key_send):
+            await_sent(qg_all.at[:, pl.ds(0, rows - runs)], send_sem.at[0])
+    await_bytes(out, out_recv.at[0])
+
+
+def settle_kernel(count, pieces, source, *refs):
+    targets, sem = refs[:count], refs[count]
+    copies = [
+        pltpu.make_async_copy(
+            source.at[at, piece], targets[at].at[piece], sem.at[at * pieces + piece]
         )
+        for at in range(count)
+        for piece in range(pieces)
+    ]
+    for copy in copies:
         copy.start()
-        pair_copies.append(copy)
-    for copy in pair_copies:
-        copy.wait_recv()
-    for dz in far_first:
-        z1 = (z + n_z - dz) % n_z
-
-        def join_step(r, carry, z1=z1):
-            row, run = z1 * runs + r, 2 * z1 + c
-            for sums, far, take, stage in (
-                (k_sum, k_far, k_take, dk_stage),
-                (v_sum, v_far, v_take, dv_stage),
-            ):
-                total = total_of(sums, far, run, r) + take[row].astype(jnp.float32)
-                stage[row] = total.astype(jnp.bfloat16)
-            return carry
-
-        lax.fori_loop(0, runs, join_step, 0)
-        hand_out(key_outs, dz)
-
-    for dz in range(1, n_z):
-        z1 = (z + n_z - dz) % n_z
-        for at, stage, out in row_outs + key_outs:
-            pltpu.make_async_remote_copy(
-                src_ref=stage.at[pl.ds(z1 * runs, runs)],
-                dst_ref=out.at[:, :, columns(z1)],
-                send_sem=out_send.at[at, z1],
-                recv_sem=out_recv.at[at, z1],
-                device_id=sibling,
-                device_id_type=MESH,
-            ).wait_recv()
-    for copy in own_outs:
+    for copy in copies:
         copy.wait()
-    for copy in sends + passes + pair_copies:
-        copy.wait_send()
-
-
-def settle_kernel(count, pieces, *refs):
-    sources, targets = refs[:count], refs[count : 2 * count]
-    held, in_sem, out_sem = refs[2 * count :]
-    loads, stores = [], []
-    for at in range(count):
-        for piece in range(pieces):
-            loads.append(
-                pltpu.make_async_copy(
-                    sources[at].at[piece], held.at[at, piece], in_sem.at[at, piece]
-                )
-            )
-            stores.append(
-                pltpu.make_async_copy(
-                    held.at[at, piece], targets[at].at[piece], out_sem.at[at, piece]
-                )
-            )
-    for load in loads:
-        load.start()
-    for load, store in zip(loads, stores):
-        load.wait()
-        store.start(priority=1)
-    for store in stores:
-        store.wait()
 
 
 def by_heads(queries, keys, values, grad_out, stride_owner):
     n_head, n_blk = lax.axis_size("head"), lax.axis_size("blk")
     n_z = n_blk // 2
     rows = n_z * n_head
+    rounds = n_z - 1 + n_head.bit_length() - 1
     seq_rows, width = BLOCK * n_head, n_z * HEAD_DIM
     tile = (BLOCK, HEAD_DIM)
     low, wide = jnp.bfloat16, jnp.float32
     dma = pltpu.SemaphoreType.DMA
-    out = jax.ShapeDtypeStruct((n_head, BLOCK, width), low)
-    anywhere = pl.BlockSpec(memory_space=pl.ANY)
+    out_bytes = 8 * seq_rows * width
     arrived = pl.pallas_call(
         partial(head_kernel, n_head, n_z),
-        out_shape=(out,) * 4,
+        out_shape=pltpu.VMEM((4, n_head, BLOCK, width), low),
         in_specs=[pl.BlockSpec(memory_space=pltpu.HBM)] * 5,
-        out_specs=(anywhere,) * 4,
+        out_specs=pl.BlockSpec(memory_space=pltpu.VMEM),
         scratch_shapes=[
             pltpu.SMEM(stride_owner.shape[::-1], jnp.int32),
-            pltpu.VMEM((rows,) + tile, low),
-            pltpu.VMEM((2 * rows,) + tile, low),
-            pltpu.VMEM((2 * rows,) + tile, low),
-            pltpu.VMEM((rows,) + tile, low),
+            pltpu.VMEM((2, 2 * rows) + tile, low),
+            pltpu.VMEM((2, rows) + tile, low),
             pltpu.VMEM((2 * rows,) + tile, wide),
             pltpu.VMEM((2 * rows,) + tile, wide),
             pltpu.VMEM((rows * PICKS + 1,) + tile, low),
             pltpu.VMEM((rows * PICKS + 1,) + tile, low),
-        ]
-        + [pltpu.VMEM((rows,) + tile, low)] * 8
-        + [
-            dma((4, rows)),
-            dma((4, rows)),
-            dma((2, rows)),
-            dma((2, rows)),
-            dma((5,)),
-            dma((4, n_z)),
-            dma((4, n_z)),
-            dma((4,)),
-            dma((2,)),
-            dma((2,)),
+            pltpu.VMEM((4, rows) + tile, low),
+            pltpu.VMEM((2, rows) + tile, low),
+            pltpu.VMEM((2, rows) + tile, low),
+            dma((1,)),
+            dma((1,)),
+            dma((n_z,)),
+            dma((1,)),
+            dma((n_z,)),
+            dma((n_z,)),
+            dma((n_z,)),
+            dma((1,)),
+            dma((1,)),
+            dma((1,)),
+            dma((1,)),
+            dma((1,)),
+            pltpu.SemaphoreType.REGULAR((max(1, rounds - 1),)),
         ],
         compiler_params=pltpu.CompilerParams(
-            collective_id=0, has_side_effects=True, vmem_limit_bytes=67043328
+            collective_id=0, has_side_effects=True, vmem_limit_bytes=67043328 - out_bytes
         ),
     )(stride_owner.T, queries, keys, values, grad_out)
+    out = jax.ShapeDtypeStruct((n_head, BLOCK, width), low)
     settled = pl.pallas_call(
         partial(settle_kernel, 4, n_head),
         out_shape=(out,) * 4,
-        in_specs=[pl.BlockSpec(memory_space=pl.ANY)] * 4,
+        in_specs=[pl.BlockSpec(memory_space=pltpu.VMEM)],
         out_specs=(pl.BlockSpec(memory_space=pl.ANY),) * 4,
-        scratch_shapes=[
-            pltpu.VMEM((4, n_head, BLOCK, width), low),
-            dma((4, n_head)),
-            dma((4, n_head)),
-        ],
-        compiler_params=pltpu.CompilerParams(vmem_limit_bytes=67043328),
-    )(*arrived)
+        scratch_shapes=[dma((4 * n_head,))],
+        compiler_params=pltpu.CompilerParams(vmem_limit_bytes=8 << 20),
+    )(arrived)
     return tuple(part.reshape(seq_rows, width) for part in settled)
 
 
 def on_device(queries, keys, values, grad_out, stride_owner):
     n_head, n_blk = lax.axis_size("head"), lax.axis_size("blk")
     rows, width = queries.shape
-    if rows == BLOCK and n_blk % 2 == 0 and width == n_head * (n_blk // 2) * HEAD_DIM:
+    whole_heads = n_blk % 2 == 0 and width == n_head * (n_blk // 2) * HEAD_DIM
+    if rows == BLOCK and whole_heads and n_head & (n_head - 1) == 0:
         return by_heads(queries, keys, values, grad_out, stride_owner)
     return by_runs(queries, keys, values, grad_out, stride_owner)
 

time: 102 us -> 96.6 us (0.947)
  Pallas kernels: 101 us -> 95.5 us
    pallas_call x1, Pallas kernels: 98.5 us -> 94.1 us  [by_heads(): pl.pallas_call(partial(head_kernel, n_head, n_z), out_shape=pltpu.VMEM((4...]
    pallas_call x1, Pallas kernels: 2.57 us -> 1.44 us  [by_heads(): pl.pallas_call(partial(settle_kernel, 4, n_head), out_shape=(out,) * 4, i...]
where the time goes in v1:
time: 96.6 us; the launch traced here: 96.2 us
  Pallas kernels  95.5 us (99%)
    pallas_call x1, Pallas kernels, by_heads(): pl.pallas_call(partial(head_kernel, n_head, n_z), out_shape=pltpu.VMEM((4...  94.1 us

profile of v1, /device:TPU:9, one launch (start us, length us, event | category | flops | bytes accessed | tf_op | source)
XLA Modules:
  0.0 96.2 jit_solution(8641765686357673825)
XLA Ops:
  0.6 94.1 %shard_map.84.source = bf16[4,4,128,512]{3,2,1,0:T(8,128)(2,1)S(1)} custom-call(s32[3,32]{1,0:T(4,128)} %bitcast.5, bf16[128,2048]{1,0:T(8,128)(2,1)} %q_in.1, bf16[128,2048]{1,0:T(8,128)(2,1)} %k_in.1, bf16[128,2048]{1,0:T(8,128)(2,1)} %v_in.1, bf16[128,2048]{1,0:T(8,128)(2,1)} %g_in.1), custom_call_target="tpu_custom_call" | custom-call | tf_op jit(solution)/shard_map/pallas_call | solution.py:610
  94.7 1.4 %shard_map.85 = (bf16[4,128,512]{2,1,0:T(8,128)(2,1)}, bf16[4,128,512]{2,1,0:T(8,128)(2,1)}, bf16[4,128,512]{2,1,0:T(8,128)(2,1)}, bf16[4,128,512]{2,1,0:T(8,128)(2,1)}) custom-call(bf16[4,4,128,512]{3,2,1,0:T(8,128)(2,1)S(1)} %shard_map.84.source), custom_call_target="tpu_custom_call" | custom-call | tf_op jit(solution)/shard_map/pallas_call | solution.py:645

commit v2 on v1

--- a/solution.py
+++ b/solution.py
@@ -284,16 +284,14 @@
     give,
     take,
     owner_sem,
-    kv_send,
+    in_send,
     kv_recv,
-    qg_send,
     qg_recv,
     pass_send,
     pass_recv,
     pair_send,
     pair_recv,
-    row_send,
-    key_send,
+    out_send,
     out_recv,
     near_sem,
 ):
@@ -406,11 +404,13 @@
             greet(near_sem.at[distance - 1])
         for hop, minus, flips in everyone:
             if hop == distance:
-                push_pair((k_in, v_in), kv_all, mine, kv_send, kv_recv, -minus, flips)
+                push_pair((k_in, v_in), kv_all, mine, in_send, kv_recv, -minus, flips)
+                if (-minus, flips) == (1, 0):
+                    push_pair((q_in, g_in), qg_all, my_row, in_send, qg_recv, 1, 0)
     for dz in [n_z // 2] + [d for d in range(n_z - 1, -1, -1) if d != n_z // 2]:
         for flips in range(n_head):
-            if dz + hops(flips) > 0:
-                push_pair((q_in, g_in), qg_all, my_row, qg_send, qg_recv, dz, flips)
+            if dz + hops(flips) > 0 and (dz, flips) != (1, 0):
+                push_pair((q_in, g_in), qg_all, my_row, in_send, qg_recv, dz, flips)
 
     blank = jnp.zeros((BLOCK, HEAD_DIM), jnp.float32)
 
@@ -437,24 +437,20 @@
     def run_of(dz, core):
         return 2 * ((z + n_z - dz) % n_z) + core
 
-    passes = []
     order = [0, 1, n_z - 1] + list(range(2, n_z - 1))
     for dz in order[:n_z]:
         group = kv_all.at[:, pl.ds(run_of(dz, c) * runs, runs)]
         await_bytes(group, kv_recv.at[dz])
-        copy = pltpu.make_async_remote_copy(
+        pltpu.make_async_remote_copy(
             src_ref=group,
             dst_ref=group,
-            send_sem=pass_send.at[dz],
-            recv_sem=pass_recv.at[dz],
+            send_sem=pass_send.at[0],
+            recv_sem=pass_recv.at[0],
             device_id=sibling,
             device_id_type=MESH,
-        )
-        copy.start()
-        passes.append(copy)
+        ).start()
     local[0].wait()
-    for dz in range(n_z):
-        await_bytes(kv_all.at[:, pl.ds(run_of(dz, 1 - c) * runs, runs)], pass_recv.at[dz])
+    await_bytes(qg_all, pass_recv.at[0])
 
     def contract(left, right, dims):
         return lax.dot_general(
@@ -492,7 +488,7 @@
             k_far[row * PICKS + j] = key_terms[rows].astype(jnp.bfloat16)
             v_far[row * PICKS + j] = value_terms[rows].astype(jnp.bfloat16)
 
-    def hand_out(first, send_sem, dz):
+    def hand_out(first, dz):
         z2 = (z + n_z - dz) % n_z
         source = stage.at[pl.ds(first, 2), pl.ds(z2 * runs, runs)]
         target = out.at[pl.ds(first, 2), :, :, columns(z)]
@@ -502,7 +498,7 @@
             pltpu.make_async_remote_copy(
                 src_ref=source,
                 dst_ref=target,
-                send_sem=send_sem.at[0],
+                send_sem=out_send.at[0],
                 recv_sem=out_recv.at[0],
                 device_id={"head": head, "blk": 2 * z2 + c},
                 device_id_type=MESH,
@@ -518,7 +514,7 @@
             return carry
 
         lax.fori_loop(0, runs, step, 0)
-        hand_out(0, row_send, dz)
+        hand_out(0, dz)
 
     def total_of(sums, far, run, r):
         total = sums[run * runs + r]
@@ -559,7 +555,7 @@
             return carry
 
         lax.fori_loop(0, runs, join_step, 0)
-        hand_out(2, key_send, dz)
+        hand_out(2, dz)
 
     def await_sent(ref, sem):
         pltpu.make_async_remote_copy(
@@ -572,13 +568,11 @@
         ).wait_send()
 
     rows = n_z * runs
-    for copy in passes + [pair]:
-        copy.wait_send()
-    await_sent(kv_all.at[:, pl.ds(0, rows - 1)], kv_send.at[0])
-    await_sent(qg_all.at[:, pl.ds(0, rows - 1)], qg_send.at[0])
+    pair.wait_send()
+    await_sent(qg_all, pass_send.at[0])
+    await_sent(kv_all.at[:, pl.ds(0, 2 * (rows - 1))], in_send.at[0])
     if n_z > 1:
-        for send_sem in (row_send, key_send):
-            await_sent(qg_all.at[:, pl.ds(0, rows - runs)], send_sem.at[0])
+        await_sent(kv_all.at[:, pl.ds(0, 2 * (rows - runs))], out_send.at[0])
     await_bytes(out, out_recv.at[0])
 
 
@@ -586,15 +580,14 @@
     targets, sem = refs[:count], refs[count]
     copies = [
         pltpu.make_async_copy(
-            source.at[at, piece], targets[at].at[piece], sem.at[at * pieces + piece]
+            source.at[at, piece], targets[at].at[piece], sem.at[0]
         )
         for at in range(count)
         for piece in range(pieces)
     ]
     for copy in copies:
         copy.start()
-    for copy in copies:
-        copy.wait()
+    pltpu.make_async_copy(source, source, sem.at[0]).wait()
 
 
 def by_heads(queries, keys, values, grad_out, stride_owner):
@@ -626,10 +619,8 @@
             dma((1,)),
             dma((1,)),
             dma((n_z,)),
-            dma((1,)),
             dma((n_z,)),
-            dma((n_z,)),
-            dma((n_z,)),
+            dma((1,)),
             dma((1,)),
             dma((1,)),
             dma((1,)),
@@ -647,7 +638,7 @@
         out_shape=(out,) * 4,
         in_specs=[pl.BlockSpec(memory_space=pltpu.VMEM)],
         out_specs=(pl.BlockSpec(memory_space=pl.ANY),) * 4,
-        scratch_shapes=[dma((4 * n_head,))],
+        scratch_shapes=[dma((1,))],
         compiler_params=pltpu.CompilerParams(vmem_limit_bytes=8 << 20),
     )(arrived)
     return tuple(part.reshape(seq_rows, width) for part in settled)

time: 96.6 us -> 96.2 us (level)
  no operation moved by 1% of the time
where the time goes in v2:
time: 96.2 us; the launch traced here: 96.1 us
  Pallas kernels  95.4 us (99%)
    pallas_call x1, Pallas kernels, by_heads(): pl.pallas_call(partial(head_kernel, n_head, n_z), out_shape=pltpu.VMEM((4...  94.1 us

profile of v2, /device:TPU:9, one launch (start us, length us, event | category | flops | bytes accessed | tf_op | source)
XLA Modules:
  0.0 96.1 jit_solution(14203422973000966779)
XLA Ops:
  0.6 94.1 %shard_map.84.source = bf16[4,4,128,512]{3,2,1,0:T(8,128)(2,1)S(1)} custom-call(s32[3,32]{1,0:T(4,128)} %bitcast.5, bf16[128,2048]{1,0:T(8,128)(2,1)} %q_in.1, bf16[128,2048]{1,0:T(8,128)(2,1)} %k_in.1, bf16[128,2048]{1,0:T(8,128)(2,1)} %v_in.1, bf16[128,2048]{1,0:T(8,128)(2,1)} %g_in.1), custom_call_target="tpu_custom_call" | custom-call | tf_op jit(solution)/shard_map/pallas_call | solution.py:603
  94.8 1.3 %shard_map.85 = (bf16[4,128,512]{2,1,0:T(8,128)(2,1)}, bf16[4,128,512]{2,1,0:T(8,128)(2,1)}, bf16[4,128,512]{2,1,0:T(8,128)(2,1)}, bf16[4,128,512]{2,1,0:T(8,128)(2,1)}) custom-call(bf16[4,4,128,512]{3,2,1,0:T(8,128)(2,1)S(1)} %shard_map.84.source), custom_call_target="tpu_custom_call" | custom-call | tf_op jit(solution)/shard_map/pallas_call | solution.py:636

commit v3 on v2

--- a/solution.py
+++ b/solution.py
@@ -262,6 +262,52 @@
         grad_keys,
         grad_values,
     )
+
+
+def head_bits(n_head):
+    return [1 << bit for bit in range(n_head.bit_length() - 1)]
+
+
+def neighbours(n_head, n_z, at_z):
+    beside = [(at_z, flip, 0) for flip in head_bits(n_head)] + [(at_z, 0, 1)]
+    return beside + [(z2, 0, 0) for z2 in (at_z - 1, at_z + 1) if 0 <= z2 < n_z]
+
+
+def seen_from(peer, at_z):
+    return (at_z, peer[1], peer[2])
+
+
+def entry_rounds(n_head, n_z):
+    middle = n_z // 2
+    hears, knows = [], []
+    near = [neighbours(n_head, n_z, at_z) for at_z in range(n_z)]
+    first = [set(near[at_z]) for at_z in range(n_z)]
+    if middle:
+        first[middle] = {(middle - 1, 0, 0)}
+    hears.append(first)
+    knows.append([{(at_z, 0, 0)} | first[at_z] for at_z in range(n_z)])
+    reached = [
+        {(z2, flips, 0) for z2 in range(n_z) for flips in range(n_head)} | {(at_z, 0, 1)}
+        for at_z in range(n_z)
+    ]
+    while any(want - known for want, known in zip(reached, knows[-1])):
+        known = knows[-1]
+        heard = [
+            {p for p in near[at_z] if seen_from(p, at_z) in known[p[0]]} for at_z in range(n_z)
+        ]
+        hears.append(heard)
+        knows.append(
+            [
+                known[at_z].union(
+                    *(
+                        {(k[0], k[1] ^ p[1], k[2] ^ p[2]) for k in known[p[0]]}
+                        for p in heard[at_z]
+                    )
+                )
+                for at_z in range(n_z)
+            ]
+        )
+    return hears, knows
 
 
 def head_kernel(
@@ -310,107 +356,91 @@
     def columns(head_id):
         return pl.ds(pl.multiple_of(head_id * HEAD_DIM, HEAD_DIM), HEAD_DIM)
 
-    bits = [1 << b for b in range(n_head.bit_length() - 1)]
-
-    def greet(sem):
-        for flip in bits:
-            pl.semaphore_signal(
-                sem,
-                inc=1,
-                device_id={"head": flipped(head, flip), "blk": blk},
-                device_id_type=MESH,
-            )
-        pl.semaphore_signal(sem, inc=1, device_id=sibling, device_id_type=MESH)
-
-        @pl.when(z > 0)
-        def _():
-            pl.semaphore_signal(
-                sem, inc=1, device_id={"head": head, "blk": blk - 2}, device_id_type=MESH
-            )
-
-        @pl.when(z < n_z - 1)
-        def _():
-            pl.semaphore_signal(
-                sem, inc=1, device_id={"head": head, "blk": blk + 2}, device_id_type=MESH
-            )
-
-    def flipped(head_id, flips):
-        moved = head_id
+    bits = head_bits(n_head)
+    hears, knows = entry_rounds(n_head, n_z)
+    barrier = pltpu.get_barrier_semaphore()
+
+    def flipped(flips):
+        moved = head
         for flip in bits:
             if flips & flip:
-                moved = moved + flip - 2 * flip * ((head_id // flip) % 2)
+                moved = moved + flip - 2 * flip * ((head // flip) % 2)
         return moved
 
-    def hear(sem):
-        ends = len(bits) + 1 + (z > 0).astype(jnp.int32) + (z < n_z - 1).astype(jnp.int32)
-        pl.semaphore_wait(sem, ends)
-
-    barrier = pltpu.get_barrier_semaphore()
-    greet(barrier)
-
-    local = [pltpu.make_async_copy(owner_in, owner_ref, owner_sem.at[0])]
-    for at, source in enumerate((k_in, v_in)):
-        local.append(
-            pltpu.make_async_copy(
-                source.at[:, columns(my_head)], kv_all.at[at, mine], kv_recv.at[0]
-            )
-        )
-    for at, source in enumerate((q_in, g_in)):
-        local.append(
-            pltpu.make_async_copy(
-                source.at[:, columns(my_head)], qg_all.at[at, my_row], qg_recv.at[0]
-            )
-        )
-    for copy in local:
-        copy.start()
-
-    def push(at, source, target, slot, send_sem, recv_sem, z2, flips):
-        h2 = flipped(head, flips)
-        pltpu.make_async_remote_copy(
-            src_ref=source.at[:, columns(h2 * n_z + z2)],
-            dst_ref=target.at[at, slot],
-            send_sem=send_sem.at[0],
-            recv_sem=recv_sem,
-            device_id={"head": h2, "blk": 2 * z2 + c},
-            device_id_type=MESH,
-        ).start()
-
-    def push_pair(sources, target, slot, send_sem, recv_sem, dz, flips):
-        for sign in (1, -1) if dz else (1,):
-            z2 = z + sign * dz
-
-            @pl.when((z2 >= 0) & (z2 < n_z))
-            def _(z2=z2):
-                arrive = recv_sem.at[(z2 + n_z - z) % n_z]
-                for at, source in enumerate(sources):
-                    push(at, source, target, slot, send_sem, arrive, z2, flips)
-
-    def hops(flips):
-        return sum(1 for flip in bits if flips & flip)
-
-    everyone = sorted(
-        (dz + hops(flips), -dz, flips)
-        for dz in range(n_z)
-        for flips in range(n_head)
-        if dz + hops(flips) > 0
-    )
-    rounds = n_z - 1 + len(bits)
-    for distance in range(1, rounds + 1):
-        if distance == 1:
-            hear(barrier)
-        else:
-            hear(near_sem.at[distance - 2])
-        if distance < rounds:
-            greet(near_sem.at[distance - 1])
-        for hop, minus, flips in everyone:
-            if hop == distance:
-                push_pair((k_in, v_in), kv_all, mine, in_send, kv_recv, -minus, flips)
-                if (-minus, flips) == (1, 0):
-                    push_pair((q_in, g_in), qg_all, my_row, in_send, qg_recv, 1, 0)
-    for dz in [n_z // 2] + [d for d in range(n_z - 1, -1, -1) if d != n_z // 2]:
-        for flips in range(n_head):
-            if dz + hops(flips) > 0 and (dz, flips) != (1, 0):
-                push_pair((q_in, g_in), qg_all, my_row, in_send, qg_recv, dz, flips)
+    def place(peer):
+        at_z, flips, other = peer
+        return {"head": flipped(flips), "blk": 2 * at_z + (1 - c if other else c)}
+
+    def greet(at_z, step):
+        sem = barrier if step == 0 else near_sem.at[step - 1]
+        for peer in neighbours(n_head, n_z, at_z):
+            if seen_from(peer, at_z) in hears[step][peer[0]]:
+                pl.semaphore_signal(sem, inc=1, device_id=place(peer), device_id_type=MESH)
+
+    def hear(at_z, step):
+        sem = barrier if step == 0 else near_sem.at[step - 1]
+        if hears[step][at_z]:
+            pl.semaphore_wait(sem, len(hears[step][at_z]))
+
+    def push(sources, target, slot, recv_sem, at_z, peer):
+        z2, flips, _ = peer
+        for at, source in enumerate(sources):
+            pltpu.make_async_remote_copy(
+                src_ref=source.at[:, columns(flipped(flips) * n_z + z2)],
+                dst_ref=target.at[at, slot],
+                send_sem=in_send.at[0],
+                recv_sem=recv_sem.at[(z2 + n_z - at_z) % n_z],
+                device_id=place(peer),
+                device_id_type=MESH,
+            ).start()
+
+    def crosses(at_z, peer):
+        return (at_z < n_z // 2) != (peer[0] < n_z // 2)
+
+    def urgency(at_z, peer):
+        hops = abs(peer[0] - at_z) + bin(peer[1]).count("1")
+        return (not crosses(at_z, peer), hops, peer)
+
+    def enter(at_z):
+        greet(at_z, 0)
+        local = [pltpu.make_async_copy(owner_in, owner_ref, owner_sem.at[0])]
+        for sources, target, slot, sem in (
+            ((k_in, v_in), kv_all, mine, kv_recv),
+            ((q_in, g_in), qg_all, my_row, qg_recv),
+        ):
+            for at, source in enumerate(sources):
+                local.append(
+                    pltpu.make_async_copy(
+                        source.at[:, columns(my_head)], target.at[at, slot], sem.at[0]
+                    )
+                )
+        for copy in local:
+            copy.start()
+        early = []
+        met = {(at_z, 0, 0)}
+        for step in range(len(hears)):
+            hear(at_z, step)
+            fresh = [p for p in knows[step][at_z] - met if not p[2]]
+            met |= knows[step][at_z]
+            fresh.sort(key=partial(urgency, at_z))
+            first = [p for p in fresh if step == 0 and crosses(at_z, p)]
+            for peer in first:
+                push((k_in, v_in), kv_all, mine, kv_recv, at_z, peer)
+                push((q_in, g_in), qg_all, my_row, qg_recv, at_z, peer)
+            early += first
+            if step + 1 < len(hears):
+                greet(at_z, step + 1)
+            for peer in fresh:
+                if peer not in first:
+                    push((k_in, v_in), kv_all, mine, kv_recv, at_z, peer)
+        late = [p for p in met if not p[2] and p[:2] != (at_z, 0) and p not in early]
+        for dz in [n_z // 2] + [d for d in range(n_z - 1, -1, -1) if d != n_z // 2]:
+            for peer in sorted(late, key=partial(urgency, at_z)):
+                if abs(peer[0] - at_z) == dz:
+                    push((q_in, g_in), qg_all, my_row, qg_recv, at_z, peer)
+
+    for at_z in range(n_z):
+        pl.when(z == at_z)(partial(enter, at_z))
 
     blank = jnp.zeros((BLOCK, HEAD_DIM), jnp.float32)
 
@@ -449,7 +479,7 @@
             device_id=sibling,
             device_id_type=MESH,
         ).start()
-    local[0].wait()
+    pltpu.make_async_copy(owner_in, owner_ref, owner_sem.at[0]).wait()
     await_bytes(qg_all, pass_recv.at[0])
 
     def contract(left, right, dims):
@@ -594,7 +624,7 @@
     n_head, n_blk = lax.axis_size("head"), lax.axis_size("blk")
     n_z = n_blk // 2
     rows = n_z * n_head
-    rounds = n_z - 1 + n_head.bit_length() - 1
+    rounds = len(entry_rounds(n_head, n_z)[0])
     seq_rows, width = BLOCK * n_head, n_z * HEAD_DIM
     tile = (BLOCK, HEAD_DIM)
     low, wide = jnp.bfloat16, jnp.float32

time: 96.2 us -> 94.9 us (0.986)
  Pallas kernels: 95.4 us -> 93.4 us
    pallas_call x1, Pallas kernels: 94.1 us -> 92.1 us  [by_heads(): pl.pallas_call(partial(head_kernel, n_head, n_z), out_shape=pltpu.VMEM((4...]
where the time goes in v3:
time: 94.9 us; the launch traced here: 94.1 us
  Pallas kernels  93.4 us (98%)
    pallas_call x1, Pallas kernels, by_heads(): pl.pallas_call(partial(head_kernel, n_head, n_z), out_shape=pltpu.VMEM((4...  92.1 us

profile of v3, /device:TPU:9, one launch (start us, length us, event | category | flops | bytes accessed | tf_op | source)
XLA Modules:
  0.0 94.1 jit_solution(15092776897488679604)
XLA Ops:
  0.6 92.1 %shard_map.84.source = bf16[4,4,128,512]{3,2,1,0:T(8,128)(2,1)S(1)} custom-call(s32[3,32]{1,0:T(4,128)} %bitcast.5, bf16[128,2048]{1,0:T(8,128)(2,1)} %q_in.1, bf16[128,2048]{1,0:T(8,128)(2,1)} %k_in.1, bf16[128,2048]{1,0:T(8,128)(2,1)} %v_in.1, bf16[128,2048]{1,0:T(8,128)(2,1)} %g_in.1), custom_call_target="tpu_custom_call" | custom-call | tf_op jit(solution)/shard_map/pallas_call | solution.py:633
  92.8 1.3 %shard_map.85 = (bf16[4,128,512]{2,1,0:T(8,128)(2,1)}, bf16[4,128,512]{2,1,0:T(8,128)(2,1)}, bf16[4,128,512]{2,1,0:T(8,128)(2,1)}, bf16[4,128,512]{2,1,0:T(8,128)(2,1)}) custom-call(bf16[4,4,128,512]{3,2,1,0:T(8,128)(2,1)S(1)} %shard_map.84.source), custom_call_target="tpu_custom_call" | custom-call | tf_op jit(solution)/shard_map/pallas_call | solution.py:666

commit v4 on v3

--- a/solution.py
+++ b/solution.py
@@ -534,6 +534,17 @@
                 device_id_type=MESH,
             ).start()
 
+    def await_sent(ref, sem):
+        pltpu.make_async_remote_copy(
+            src_ref=ref,
+            dst_ref=ref,
+            send_sem=sem,
+            recv_sem=sem,
+            device_id=sibling,
+            device_id_type=MESH,
+        ).wait_send()
+
+    rows = n_z * runs
     far_first = [dz for dz in (2, 1, 3, 0) if dz < n_z] + list(range(4, n_z))
     for dz in far_first:
         z1 = (z + n_z - dz) % n_z
@@ -544,6 +555,8 @@
             return carry
 
         lax.fori_loop(0, runs, step, 0)
+        if dz == far_first[0]:
+            await_sent(kv_all.at[:, pl.ds(0, 2 * (rows - 1))], in_send.at[0])
         hand_out(0, dz)
 
     def total_of(sums, far, run, r):
@@ -587,20 +600,8 @@
         lax.fori_loop(0, runs, join_step, 0)
         hand_out(2, dz)
 
-    def await_sent(ref, sem):
-        pltpu.make_async_remote_copy(
-            src_ref=ref,
-            dst_ref=ref,
-            send_sem=sem,
-            recv_sem=sem,
-            device_id=sibling,
-            device_id_type=MESH,
-        ).wait_send()
-
-    rows = n_z * runs
     pair.wait_send()
     await_sent(qg_all, pass_send.at[0])
-    await_sent(kv_all.at[:, pl.ds(0, 2 * (rows - 1))], in_send.at[0])
     if n_z > 1:
         await_sent(kv_all.at[:, pl.ds(0, 2 * (rows - runs))], out_send.at[0])
     await_bytes(out, out_recv.at[0])

time: 94.9 us -> 94.9 us (level)
  no operation moved by 1% of the time
where the time goes in v4:
time: 94.9 us; the launch traced here: 93.7 us
  Pallas kernels  93.1 us (98%)
    pallas_call x1, Pallas kernels, by_heads(): pl.pallas_call(partial(head_kernel, n_head, n_z), out_shape=pltpu.VMEM((4...  91.8 us

profile of v4, /device:TPU:9, one launch (start us, length us, event | category | flops | bytes accessed | tf_op | source)
XLA Modules:
  0.0 93.7 jit_solution(9907171394299047566)
XLA Ops:
  0.6 91.8 %shard_map.84.source = bf16[4,4,128,512]{3,2,1,0:T(8,128)(2,1)S(1)} custom-call(s32[3,32]{1,0:T(4,128)} %bitcast.5, bf16[128,2048]{1,0:T(8,128)(2,1)} %q_in.1, bf16[128,2048]{1,0:T(8,128)(2,1)} %k_in.1, bf16[128,2048]{1,0:T(8,128)(2,1)} %v_in.1, bf16[128,2048]{1,0:T(8,128)(2,1)} %g_in.1), custom_call_target="tpu_custom_call" | custom-call | tf_op jit(solution)/shard_map/pallas_call | solution.py:634
  92.4 1.3 %shard_map.85 = (bf16[4,128,512]{2,1,0:T(8,128)(2,1)}, bf16[4,128,512]{2,1,0:T(8,128)(2,1)}, bf16[4,128,512]{2,1,0:T(8,128)(2,1)}, bf16[4,128,512]{2,1,0:T(8,128)(2,1)}) custom-call(bf16[4,4,128,512]{3,2,1,0:T(8,128)(2,1)S(1)} %shard_map.84.source), custom_call_target="tpu_custom_call" | custom-call | tf_op jit(solution)/shard_map/pallas_call | solution.py:667

commit v5 on v4

--- a/solution.py
+++ b/solution.py
@@ -522,7 +522,7 @@
         z2 = (z + n_z - dz) % n_z
         source = stage.at[pl.ds(first, 2), pl.ds(z2 * runs, runs)]
         target = out.at[pl.ds(first, 2), :, :, columns(z)]
-        if dz == 0:
+        if isinstance(dz, int) and dz == 0:
             pltpu.make_async_copy(source, target, out_recv.at[0]).start()
         else:
             pltpu.make_async_remote_copy(
@@ -587,7 +587,9 @@
     )
     pair.start()
     pair.wait_recv()
-    for dz in far_first:
+    falling = list(range(n_z - 1, -1, -1))
+    for below, above in zip(falling, far_first if n_z == 4 else falling):
+        dz = jnp.where(z < n_z // 2, below, above) if below else 0
         z1 = (z + n_z - dz) % n_z
 
         def join_step(r, carry, z1=z1):

time: 94.9 us -> 94.9 us (level)
  no operation moved by 1% of the time
where the time goes in v5:
time: 94.9 us; the launch traced here: 93.7 us
  Pallas kernels  93.1 us (98%)
    pallas_call x1, Pallas kernels, by_heads(): pl.pallas_call(partial(head_kernel, n_head, n_z), out_shape=pltpu.VMEM((4...  91.8 us

profile of v5, /device:TPU:9, one launch (start us, length us, event | category | flops | bytes accessed | tf_op | source)
XLA Modules:
  0.0 93.7 jit_solution(221863601737016519)
XLA Ops:
  0.6 91.8 %shard_map.84.source = bf16[4,4,128,512]{3,2,1,0:T(8,128)(2,1)S(1)} custom-call(s32[3,32]{1,0:T(4,128)} %bitcast.5, bf16[128,2048]{1,0:T(8,128)(2,1)} %q_in.1, bf16[128,2048]{1,0:T(8,128)(2,1)} %k_in.1, bf16[128,2048]{1,0:T(8,128)(2,1)} %v_in.1, bf16[128,2048]{1,0:T(8,128)(2,1)} %g_in.1), custom_call_target="tpu_custom_call" | custom-call | tf_op jit(solution)/shard_map/pallas_call | solution.py:636
  92.4 1.3 %shard_map.85 = (bf16[4,128,512]{2,1,0:T(8,128)(2,1)}, bf16[4,128,512]{2,1,0:T(8,128)(2,1)}, bf16[4,128,512]{2,1,0:T(8,128)(2,1)}, bf16[4,128,512]{2,1,0:T(8,128)(2,1)}) custom-call(bf16[4,4,128,512]{3,2,1,0:T(8,128)(2,1)S(1)} %shard_map.84.source), custom_call_target="tpu_custom_call" | custom-call | tf_op jit(solution)/shard_map/pallas_call | solution.py:669

commit v6 on v5

--- a/solution.py
+++ b/solution.py
@@ -335,7 +335,6 @@
     qg_recv,
     pass_send,
     pass_recv,
-    pair_send,
     pair_recv,
     out_send,
     out_recv,
@@ -580,7 +579,7 @@
     pair = pltpu.make_async_remote_copy(
         src_ref=give,
         dst_ref=take,
-        send_sem=pair_send.at[0],
+        send_sem=pass_send.at[0],
         recv_sem=pair_recv.at[0],
         device_id=sibling,
         device_id_type=MESH,
@@ -602,8 +601,7 @@
         lax.fori_loop(0, runs, join_step, 0)
         hand_out(2, dz)
 
-    pair.wait_send()
-    await_sent(qg_all, pass_send.at[0])
+    await_sent(kv_all, pass_send.at[0])
     if n_z > 1:
         await_sent(kv_all.at[:, pl.ds(0, 2 * (rows - runs))], out_send.at[0])
     await_bytes(out, out_recv.at[0])
@@ -627,11 +625,11 @@
     n_head, n_blk = lax.axis_size("head"), lax.axis_size("blk")
     n_z = n_blk // 2
     rows = n_z * n_head
-    rounds = len(entry_rounds(n_head, n_z)[0])
     seq_rows, width = BLOCK * n_head, n_z * HEAD_DIM
     tile = (BLOCK, HEAD_DIM)
     low, wide = jnp.bfloat16, jnp.float32
     dma = pltpu.SemaphoreType.DMA
+    rounds = len(entry_rounds(n_head, n_z)[0])
     out_bytes = 8 * seq_rows * width
     arrived = pl.pallas_call(
         partial(head_kernel, n_head, n_z),
@@ -658,7 +656,6 @@
             dma((1,)),
             dma((1,)),
             dma((1,)),
-            dma((1,)),
             pltpu.SemaphoreType.REGULAR((max(1, rounds - 1),)),
         ],
         compiler_params=pltpu.CompilerParams(

time: 94.9 us -> 94.9 us (level)
  no operation moved by 1% of the time
where the time goes in v6:
time: 94.9 us; the launch traced here: 93.7 us
  Pallas kernels  93.1 us (98%)
    pallas_call x1, Pallas kernels, by_heads(): pl.pallas_call(partial(head_kernel, n_head, n_z), out_shape=pltpu.VMEM((4...  91.8 us

profile of v6, /device:TPU:9, one launch (start us, length us, event | category | flops | bytes accessed | tf_op | source)
XLA Modules:
  0.0 93.7 jit_solution(17801089863292061696)
XLA Ops:
  0.6 91.8 %shard_map.84.source = bf16[4,4,128,512]{3,2,1,0:T(8,128)(2,1)S(1)} custom-call(s32[3,32]{1,0:T(4,128)} %bitcast.5, bf16[128,2048]{1,0:T(8,128)(2,1)} %q_in.1, bf16[128,2048]{1,0:T(8,128)(2,1)} %k_in.1, bf16[128,2048]{1,0:T(8,128)(2,1)} %v_in.1, bf16[128,2048]{1,0:T(8,128)(2,1)} %g_in.1), custom_call_target="tpu_custom_call" | custom-call | tf_op jit(solution)/shard_map/pallas_call | solution.py:634
  92.4 1.3 %shard_map.85 = (bf16[4,128,512]{2,1,0:T(8,128)(2,1)}, bf16[4,128,512]{2,1,0:T(8,128)(2,1)}, bf16[4,128,512]{2,1,0:T(8,128)(2,1)}, bf16[4,128,512]{2,1,0:T(8,128)(2,1)}) custom-call(bf16[4,4,128,512]{3,2,1,0:T(8,128)(2,1)S(1)} %shard_map.84.source), custom_call_target="tpu_custom_call" | custom-call | tf_op jit(solution)/shard_map/pallas_call | solution.py:666
